TPU v7x, 256 devices: a whole 4x4x8 slice. The times are simulated.
256 devices in a mesh: ctx: 16 (over x, z_lo), sec: 8 (over y, core), dp: 2 (over z_hi).
Axes of the slice: x: 4, y: 4, z: 8 (z_hi: 2, z_lo: 4; z = z_hi * 4 + z_lo), core: 2. Of those that a mesh axis runs over, the one named last changes fastest.
Arguments:
- fresh_input: bfloat16 [2, 4096, 1536], P('dp', 'ctx'), may hold values from -6 to 6
- carried: bfloat16 [8, 2, 4096, 1536], P('sec', 'dp', 'ctx'), may hold values from -6 to 6
- qkv_weight: bfloat16 [8, 1536, 4608], P('sec', ('ctx', 'dp')), as said below
- out_weight: bfloat16 [8, 1536, 1536], P('sec', ('ctx', 'dp')), may hold values from -0.15625 to 0.15625
- rate_weight: bfloat16 [8, 1536, 6], P('sec', ('ctx', 'dp')), may hold values from -0.15625 to 0.15625
- fast_state: float32 [8, 2, 3, 6, 768, 256], P('sec', 'dp', None, None, 'ctx'), may hold values from -6 to 6
Outputs:
- passed: bfloat16 [8, 2, 4096, 1536], P('sec', 'dp', 'ctx')
- new_state: float32 [8, 2, 3, 6, 768, 256], P('sec', 'dp', None, None, 'ctx')
Inputs may be any that keep to these rules, and one draw needn't show every extreme that they name: Every entry of qkv_weight is at most 6 / sqrt(1536) in magnitude.
All inputs are finite; a program needn't handle non-finite values.
Results may differ from a plain program's by a relative error of at most 0.022.
Values may be sent and summed in bfloat16 or wider, within the bound.
No kernel may reach another device: no remote copies, remote signals or barrier semaphores. Data moves between devices by JAX's collectives and lax.ppermute only.
A program may use at most 128 MiB of HBM per device.

v0:
```python
import jax
import jax.numpy as jnp
from jax import lax
from jax.sharding import Mesh
from jax.sharding import PartitionSpec as P

CTX = ("xh", "xl", "zl")
CTX_DP = CTX + ("dp",)
LANES = 128
linear_coef = 3.4445
cubic_coef = -4.775
quintic_coef = 2.0315
update_scale = 8.0
highest = lax.Precision.HIGHEST


def swish(values):
    return values * jax.nn.sigmoid(values)


def unit_rows(values):
    return values / jnp.sqrt(jnp.sum(values * values, axis=-1, keepdims=True) + 1e-06)


def swap_pair(block):
    return lax.ppermute(block, "xh", [(0, 1), (1, 0)])


def pair_shard(low, high, is_low, dim):
    kept = jnp.where(is_low, low, high)
    got = swap_pair(jnp.where(is_low, high, low))
    return jnp.concatenate([jnp.where(is_low, kept, got), jnp.where(is_low, got, kept)], axis=dim)


def polynomial(square):
    return (
        linear_coef * jnp.eye(square.shape[-1], dtype=jnp.float32)
        + cubic_coef * square
        + quintic_coef * jnp.einsum("mde,mef->mdf", square, square, precision=highest)
    )


def orthogonalize(gradient):
    square = jnp.einsum("mrd,mre->mde", gradient, gradient, precision=highest)
    inverse_norm = lax.rsqrt(jnp.trace(square, axis1=-2, axis2=-1) + 1e-06)[:, None, None]
    square = square * inverse_norm * inverse_norm
    first = polynomial(square)
    square = jnp.einsum(
        "mde,mef->mdf",
        first,
        jnp.einsum("mde,mef->mdf", square, first, precision=highest),
        precision=highest,
    )
    both = jnp.einsum("mde,mef->mdf", first, polynomial(square), precision=highest)
    return jnp.einsum("mrd,mde->mre", gradient * inverse_norm, both, precision=highest)


def local(fresh_input, carried, qkv_weight, out_weight, rate_weight, fast_state):
    is_low = lax.axis_index("xh") == 0
    sections = lax.axis_size("sec")
    heads = rate_weight.shape[2]
    head_dim = fast_state.shape[5]
    half = heads // 2
    width = half * head_dim
    rows = qkv_weight.shape[1]
    count, channels = fresh_input.shape[1:]
    w = qkv_weight[0].reshape(rows, 3, 2, width)
    rates = jnp.pad(rate_weight[0].reshape(rows, 2, half), ((0, 0), (0, 0), (0, LANES - half)))
    low, high = (
        jnp.concatenate([w[:, 0, h], w[:, 1, h], w[:, 2, h], rates[:, h]], axis=1) for h in (0, 1)
    )
    group_w = lax.all_gather(
        pair_shard(low, high, is_low, 0), ("xl", "zl", "dp"), axis=0, tiled=True
    )
    previous = fast_state[0, 0]
    shard = previous.astype(jnp.bfloat16)
    group_fast = lax.all_gather(
        pair_shard(shard[:, :half], shard[:, half:], is_low, 2), ("xl", "zl"), axis=2, tiled=True
    )
    group_out = lax.all_gather(out_weight[0], ("xl", "zl", "dp"), axis=0, tiled=True)
    is_last = lax.axis_index("sec") == sections - 1
    source = jnp.where(is_last, fresh_input[0], carried[0, 0])
    mine = lax.ppermute(source, "sec", [(i, (i + 1) % sections) for i in range(sections)])
    pairs = [
        (a * sections + i, (1 - a) * sections + (i + 1) % sections)
        for a in (0, 1)
        for i in range(sections)
    ]
    other = lax.ppermute(source, ("xh", "sec"), pairs)
    inputs = jnp.concatenate([mine, other], axis=0)
    ordered = (
        inputs.reshape(2 * count, 2, -1, rows).transpose(0, 2, 1, 3).reshape(2 * count, channels)
    )
    projected = jnp.dot(ordered, group_w, preferred_element_type=jnp.float32)
    part = lambda i: projected[:, i * width : (i + 1) * width].reshape(2 * count, half, head_dim)
    query_rows = unit_rows(swish(part(0))).astype(jnp.bfloat16)
    key_rows = unit_rows(swish(part(1))).astype(jnp.bfloat16)
    value_rows = part(2).astype(jnp.bfloat16)
    rates = jax.nn.softplus(projected[:, 3 * width : 3 * width + half])
    gate_fast, up_fast, down_fast = (group_fast[0], group_fast[1], group_fast[2])
    gate_pre = jnp.einsum("thd,hfd->htf", key_rows, gate_fast, preferred_element_type=jnp.float32)
    up_pre = jnp.einsum("thd,hfd->htf", key_rows, up_fast, preferred_element_type=jnp.float32)
    sigma = jax.nn.sigmoid(gate_pre)
    gate_act = gate_pre * sigma
    key_hidden = (gate_act * up_pre).astype(jnp.bfloat16)
    scaled_values = (rates[:, :, None] * value_rows.astype(jnp.float32)).astype(jnp.bfloat16)
    hidden_grad = -jnp.einsum(
        "thd,hfd->htf", scaled_values, down_fast, preferred_element_type=jnp.float32
    )
    up_grad = (hidden_grad * gate_act).astype(jnp.bfloat16)
    gate_grad = (hidden_grad * up_pre * sigma * (1.0 + gate_pre * (1.0 - sigma))).astype(
        jnp.bfloat16
    )
    grad_gate = jnp.einsum("htf,thd->hfd", gate_grad, key_rows, preferred_element_type=jnp.float32)
    grad_up = jnp.einsum("htf,thd->hfd", up_grad, key_rows, preferred_element_type=jnp.float32)
    grad_down = -jnp.einsum(
        "htf,thd->hfd", key_hidden, scaled_values, preferred_element_type=jnp.float32
    )
    owners = lax.axis_size(("xl", "zl"))
    spread = jnp.concatenate([grad_gate, grad_up, grad_down[: owners - 2 * half]], axis=0)
    shared = lax.psum(grad_down[owners - 2 * half :].astype(jnp.bfloat16), ("xl", "zl"))
    owned = lax.psum_scatter(
        spread.astype(jnp.bfloat16), ("xl", "zl"), scatter_dimension=0, tiled=True
    )
    gradient = jnp.concatenate([owned, shared], axis=0).astype(jnp.float32)
    current = orthogonalize(gradient).astype(jnp.bfloat16)
    shard_rows = previous.shape[2]
    blocks = current.reshape(2, owners, 2, shard_rows, head_dim)
    outgoing = blocks[0].transpose(1, 0, 2, 3).reshape(2 * owners, shard_rows, head_dim)
    arrived = lax.all_to_all(outgoing, CTX, 0, 0, tiled=True)
    arrived = arrived.reshape(2, owners, shard_rows, head_dim)
    mine_last = lax.dynamic_index_in_dim(blocks[1], lax.axis_index(("xl", "zl")), 0, keepdims=False)
    last = pair_shard(mine_last[0][None], mine_last[1][None], is_low, 0)[:, None]
    current = jnp.concatenate([arrived, last], axis=1).astype(jnp.float32)
    current = current.reshape(2, 3, half, shard_rows, head_dim).transpose(1, 0, 2, 3, 4)
    current = current.reshape(previous.shape)
    stepped = previous - update_scale * current
    rescale = jnp.sqrt(jnp.mean(previous * previous, axis=-1, keepdims=True) + 1e-06) * lax.rsqrt(
        jnp.mean(stepped * stepped, axis=-1, keepdims=True) + 1e-06
    )
    new_state = (stepped * rescale)[None, None]
    gate_query = jnp.einsum(
        "thd,hfd->htf", query_rows, gate_fast, preferred_element_type=jnp.float32
    )
    up_query = jnp.einsum("thd,hfd->htf", query_rows, up_fast, preferred_element_type=jnp.float32)
    hidden = (swish(gate_query) * up_query).astype(jnp.bfloat16)
    mixture = jnp.einsum("htf,hfd->thd", hidden, down_fast, preferred_element_type=jnp.float32)
    head_out = (
        mixture * lax.rsqrt(jnp.mean(mixture * mixture, axis=-1, keepdims=True) + 1e-05)
    ).astype(jnp.bfloat16)
    branch_out = jnp.dot(
        head_out.reshape(2 * count, width), group_out, preferred_element_type=jnp.float32
    )
    from_pair = swap_pair(branch_out[count:].astype(jnp.bfloat16))
    passed = (
        mine.astype(jnp.float32) + (branch_out[:count] + from_pair.astype(jnp.float32))
    ).astype(jnp.bfloat16)
    return (passed[None, None], new_state)


def solution(mesh):
    shape = (2, 2, 4, mesh.shape["sec"], mesh.shape["dp"])
    split = Mesh(mesh.devices.reshape(shape), ("xh", "xl", "zl", "sec", "dp"))
    in_specs = (
        P("dp", CTX, None),
        P("sec", "dp", CTX, None),
        P("sec", CTX_DP, None),
        P("sec", CTX_DP, None),
        P("sec", CTX_DP, None),
        P("sec", "dp", None, None, CTX, None),
    )
    out_specs = (P("sec", "dp", CTX, None), P("sec", "dp", None, None, CTX, None))
    return jax.shard_map(local, mesh=split, in_specs=in_specs, out_specs=out_specs, check_vma=False)
```

profile of v0, /device:TPU:8, one launch (start us, length us, event | category | flops | bytes accessed | tf_op | source)
XLA Modules:
  0.0 848.2 jit_solution(16667933280861583742)
XLA Ops:
  8.0 1.1 reshape_squeeze.6
  10.0 3.1 collective-permute-start.3
  13.1 5.9 collective-permute-done.3
  19.1 0.8 pad_maximum_fusion.2
  20.1 3.1 collective-permute-start.1
  23.2 4.8 collective-permute-done.1
  28.1 0.9 pad_maximum_fusion.3
  29.1 0.8 collective-permute-start.2
  29.9 3.4 collective-permute-start
  33.4 19.9 %collective-permute-done.2 = bf16[256,1536]{1,0:T(8,128)(2,1)S(1)} collective-permute-done((bf16[256,1536]{1,0:T(8,128)(2,1)S(1)}, bf16[256,1536]{1,0:T(8,128)(2,1)S(1)}, u32[]{:S(2)}, u32[]{:S(2)}) %collective-permute-start.2) | collective-permute-done | bytes 786464 | tf_op jit(solution)/shard_map/ppermute | solution.py:89
  53.4 0.9 copy-done.7
  54.3 0.7 copy.174
  55.2 358.9 %all-gather.7.cloned.1.call-done = bf16[1536,2432]{1,0:T(8,128)(2,1)} async-done(((bf16[96,2432]{1,0:T(8,128)(2,1)}), bf16[1536,2432]{1,0:T(8,128)(2,1)}) %all-gather.7.cloned.1.call-update) | async-done | bytes 7471120 | tf_op jit(solution)/shard_map/all_gather | solution.py:72
  414.1 6.8 fusion.47
  420.9 1.9 fusion.44
  423.2 1.9 copy.184
  425.5 1.6 copy.182
  427.3 71.4 %all-gather.5.cloned.1.call-done = bf16[3,3,768,256]{3,2,1,0:T(8,128)(2,1)} async-done(((bf16[3,3,96,256]{3,2,1,0:T(8,128)(2,1)}), bf16[3,3,768,256]{3,2,1,0:T(8,128)(2,1)}) %all-gather.5.cloned.1.call-update) | async-done | bytes 3538960 | tf_op jit(solution)/shard_map/all_gather | solution.py:77
  498.6 2.5 fusion.26
  501.1 1.1 fusion.24
  502.5 1.9 negate_convert_fusion
  504.4 0.9 fusion.23
  505.4 4.6 fusion.17
  510.0 5.3 fusion.16
  515.3 1.9 pad_maximum_fusion
  517.6 0.9 copy-done.6
  518.5 0.8 slice.126
  520.2 4.5 fusion.25
  524.7 5.7 fusion.11
  530.3 1.1 fusion.12
  531.5 115.1 %all-gather.9.cloned.1.call-done = bf16[1,768,1536]{2,1,0:T(8,128)(2,1)} async-done(((bf16[1,48,1536]{2,1,0:T(8,128)(2,1)}), bf16[1,768,1536]{2,1,0:T(8,128)(2,1)}) %all-gather.9.cloned.1.call-update) | async-done | bytes 2359312 | tf_op jit(solution)/shard_map/all_gather | solution.py:80
  646.5 3.3 fusion.3
  649.8 1.0 slice.169
  650.8 75.1 %reduce-scatter.2.cloned.1.call-done = bf16[1,768,256]{2,1,0:T(8,128)(2,1)} async-done(((bf16[8,768,256]{2,1,0:T(8,128)(2,1)}), bf16[1,768,256]{2,1,0:T(8,128)(2,1)}) %reduce-scatter.2.cloned.1.call-update) | async-done | bytes 393232 | tf_op jit(solution)/shard_map/reduce_scatter | solution.py:122
  725.9 1.8 constant_dynamic-update-slice_fusion.1
  727.7 84.6 %all-reduce.3.cloned.1.call-done = bf16[1,768,256]{2,1,0:T(8,128)(2,1)} async-done(((bf16[1,768,256]{2,1,0:T(8,128)(2,1)}), bf16[1,768,256]{2,1,0:T(8,128)(2,1)}) %all-reduce.3.cloned.1.call-update) | async-done | bytes 393232 | tf_op jit(solution)/shard_map/psum | solution.py:121
  812.3 1.8 constant_dynamic-update-slice_fusion
  814.1 1.9 select_reduce_fusion
  816.1 0.8 fusion.22
  818.3 0.7 fusion.21
  819.6 1.6 fusion.18
  822.0 2.7 collective-permute-start.5
  824.7 0.8 copy.194
  825.5 3.6 all-to-all-start
  829.1 2.5 fusion.32
  831.6 0.8 bitcast_select_fusion.2
  832.4 7.5 all-to-all-done
  840.5 1.1 subtract_multiply_fusion
  (77 shorter events, 8.2 us)
Async XLA Ops:
  7.2 407.0 %all-gather.7.cloned.1.call-start = ((), (), s32[]{:S(2)}) async-start(), calls=%async_computation.3 | async-start | bytes 7938048 | tf_op jit(solution)/shard_map/all_gather | solution.py:72
  9.9 10.1 %copy-start.1 = (f32[1,1,3,6,48,256]{5,4,3,2,1,0:T(8,128)S(1)}, f32[1,1,3,6,48,256]{5,4,3,2,1,0:T(8,128)}, u32[]{:S(2)}) copy-start(f32[1,1,3,6,48,256]{5,4,3,2,1,0:T(8,128)} %param.11) | copy-start | bytes 2654212
  10.0 9.0 %collective-permute-start.3 = (bf16[48,2432]{1,0:T(8,128)(2,1)S(1)}, bf16[48,2432]{1,0:T(8,128)(2,1)S(1)}, u32[]{:S(2)}, u32[]{:S(2)}) collective-permute-start(bf16[48,2432]{1,0:T(8,128)(2,1)S(1)} %broadcast_select_fusion.2), channel_id=1, source_target_pairs={{0,128},{128,0},{1,129},{129,1},{2,130},{130,2},{3,131},{131,3},{4... | collective-permute-start | bytes 700424 | tf_op jit(solution)/shard_map/ppermute | solution.py:26
  19.9 478.7 %all-gather.5.cloned.1.call-start = ((), (), s32[]{:S(2)}) async-start(), calls=%async_computation.2 | async-start | bytes 3981312 | tf_op jit(solution)/shard_map/all_gather | solution.py:77
  20.0 9.0 %copy-start.8 = (bf16[1,1,256,1536]{3,2,1,0:T(8,128)(2,1)S(1)}, bf16[1,1,256,1536]{3,2,1,0:T(8,128)(2,1)}, u32[]{:S(2)}) copy-start(bf16[1,1,256,1536]{3,2,1,0:T(8,128)(2,1)} %param.7) | copy-start | bytes 2359300
  20.1 9.0 %copy-start.9 = (bf16[1,256,1536]{2,1,0:T(8,128)(2,1)S(1)}, bf16[1,256,1536]{2,1,0:T(8,128)(2,1)}, u32[]{:S(2)}) copy-start(bf16[1,256,1536]{2,1,0:T(8,128)(2,1)} %param.6) | copy-start | bytes 2359300
  20.1 7.9 collective-permute-start.1
  28.9 617.6 %all-gather.9.cloned.1.call-start = ((), (), s32[]{:S(2)}) async-start(), calls=%async_computation.6 | async-start | bytes 2506752 | tf_op jit(solution)/shard_map/all_gather | solution.py:80
  29.1 24.2 %collective-permute-start.2 = (bf16[256,1536]{1,0:T(8,128)(2,1)S(1)}, bf16[256,1536]{1,0:T(8,128)(2,1)S(1)}, u32[]{:S(2)}, u32[]{:S(2)}) collective-permute-start(bf16[256,1536]{1,0:T(8,128)(2,1)S(1)} %bitcast_select_fusion), channel_id=1, source_target_pairs={{0,130},{2,132},{4,134},{6,136},{8,138},{10,140},{12,142},{14,128}... | collective-permute-start | bytes 2359304 | tf_op jit(solution)/shard_map/ppermute | solution.py:89
  29.9 23.4 %collective-permute-start = (bf16[256,1536]{1,0:T(8,128)(2,1)S(1)}, bf16[256,1536]{1,0:T(8,128)(2,1)S(1)}, u32[]{:S(2)}, u32[]{:S(2)}) collective-permute-start(bf16[256,1536]{1,0:T(8,128)(2,1)S(1)} %bitcast_select_fusion), channel_id=1, source_target_pairs={{0,2},{2,4},{4,6},{6,8},{8,10},{10,12},{12,14},{14,0},{1,3},{3,5},... | collective-permute-start | bytes 2359304 | tf_op jit(solution)/shard_map/ppermute | solution.py:83
  33.4 692.6 %reduce-scatter.2.cloned.1.call-start = ((), (), s32[]{:S(2)}) async-start(), calls=%async_computation.4 | async-start | bytes 3538944 | tf_op jit(solution)/shard_map/reduce_scatter | solution.py:122
  53.4 0.9 copy-start.7
  498.6 2.5 copy-start.11
  501.1 1.4 copy-start.4
  502.2 2.2 copy-start.12
  504.4 1.0 copy-start.5
  510.0 5.3 slice-start
  517.2 1.3 copy-start.6
  517.2 2.1 copy-start.3
  517.2 295.1 %all-reduce.3.cloned.1.call-start = ((), (), s32[]{:S(2)}) async-start(), calls=%async_computation.5 | async-start | bytes 786432 | tf_op jit(solution)/shard_map/psum | solution.py:121
  650.8 178.3 %collective-permute-start.4 = (bf16[256,1536]{1,0:T(8,128)(2,1)}, bf16[256,1536]{1,0:T(8,128)(2,1)}, u32[]{:S(2)}, u32[]{:S(2)}) collective-permute-start(bf16[256,1536]{1,0:T(8,128)(2,1)} %slice.169), channel_id=1, source_target_pairs={{0,128},{128,0},{1,129},{129,1},{2,130},{130,2},{3,131},{131,3},{4... | collective-permute-start | bytes 2359304 | tf_op jit(solution)/shard_map/ppermute | solution.py:26
  818.3 1.4 copy-start
  821.3 4.2 copy-start.10
  822.0 9.6 %collective-permute-start.5 = (bf16[1,48,256]{2,1,0:T(8,128)(2,1)}, bf16[1,48,256]{2,1,0:T(8,128)(2,1)}, u32[]{:S(2)}, u32[]{:S(2)}) collective-permute-start(bf16[1,48,256]{2,1,0:T(8,128)(2,1)} %select_bitcast_fusion), channel_id=1, source_target_pairs={{0,128},{128,0},{1,129},{129,1},{2,130},{130,2},{3,131},{131,3},{4... | collective-permute-start | bytes 73736 | tf_op jit(solution)/shard_map/ppermute | solution.py:26
  825.5 14.4 %all-to-all-start = ((bf16[16,48,256]{2,1,0:T(8,128)(2,1)}), bf16[16,48,256]{2,1,0:T(8,128)(2,1)S(1)}, u32[]{:S(2)}, u32[]{:S(2)}) async-start(bf16[16,48,256]{2,1,0:T(8,128)(2,1)} %bitcast.20), calls=%async_computation.1 | async-start | bytes 786432 | tf_op jit(solution)/shard_map/all_to_all | solution.py:130
  832.4 7.7 copy-start.2
Sparse Core Ops, SparseCore 0:
  20.0 394.0 all-gather.6
  415.9 82.6 all-gather.4
  500.4 146.0 all-gather.8
  648.9 76.9 reduce-scatter.1
  728.4 83.8 all-reduce.2
where the time goes:
time: 849 us; the launch traced here: 848 us
  waiting for transfers between devices  743 us (88%)
  matrix products  43.5 us (5%)
  local copies, waits for them, and re-layouts  17.9 us (2%)
  starting transfers between devices  17.1 us (2%)
  between operations  14.3 us (2%)
  other arithmetic  12 us (1%)
    all_gather x1, waiting for transfers between devices, local(): lax.all_gather(pair_shard(low, high, is_low, 0), ('xl', 'zl', 'dp'), axis...  359 us
    all_gather x1, waiting for transfers between devices, local(): lax.all_gather(out_weight[0], ('xl', 'zl', 'dp'), axis=0, tiled=True)  115 us
    psum x1, waiting for transfers between devices, local(): lax.psum(grad_down[owners - 2 * half:].astype(jnp.bfloat16), ('xl', 'zl'))  84.6 us
    reduce_scatter x1, waiting for transfers between devices, local(): lax.psum_scatter(spread.astype(jnp.bfloat16), ('xl', 'zl'), scatter_dimen...  75.1 us
    all_gather x1, waiting for transfers between devices, local(): lax.all_gather(pair_shard(shard[:, :half], shard[:, half:], is_low, 2), (...  71.4 us
    ppermute x1, waiting for transfers between devices, local(): other = lax.ppermute(source, ('xh', 'sec'), pairs)  19.9 us
  transfers between devices with their start and end apart: 12, of which 9 were waited for; matrix products, arithmetic and copies ran while one was open for 8% of the time, Pallas kernels for 0%

commit v1 on v0

--- a/solution.py
+++ b/solution.py
@@ -69,8 +69,14 @@
     low, high = (
         jnp.concatenate([w[:, 0, h], w[:, 1, h], w[:, 2, h], rates[:, h]], axis=1) for h in (0, 1)
     )
-    group_w = lax.all_gather(
-        pair_shard(low, high, is_low, 0), ("xl", "zl", "dp"), axis=0, tiled=True
+    group_w = jnp.concatenate(
+        lax.all_to_all(
+            jnp.stack([pair_shard(low, high, is_low, 0)] * lax.axis_size(("xl", "zl", "dp"))),
+            ("xl", "zl", "dp"),
+            0,
+            0,
+        ),
+        axis=0,
     )
     previous = fast_state[0, 0]
     shard = previous.astype(jnp.bfloat16)

time: 849 us -> 631 us (0.74)
  waiting for transfers between devices: 743 us -> 512 us
  starting transfers between devices: 17.1 us -> 27.3 us
    all_gather x1 -> x0, waiting for transfers between devices: 359 us -> none  [local(): lax.all_gather(pair_shard(low, high, is_low, 0), ('xl', 'zl', 'dp'), axis...]
    all_to_all x0 -> x1, waiting for transfers between devices: none -> 157 us  [local(): lax.all_to_all(jnp.stack([pair_shard(low, high, is_low, 0)] * lax.axis_si...]
    all_gather x1, waiting for transfers between devices: 71.4 us -> 0.01 us  [local(): lax.all_gather(pair_shard(shard[:, :half], shard[:, half:], is_low, 2), (...]
    ppermute x4, waiting for transfers between devices: 10.7 us -> 60 us  [swap_pair(): return lax.ppermute(block, 'xh', [(0, 1), (1, 0)])]
    all_to_all x0 -> x1, starting transfers between devices: none -> 9.67 us  [local(): lax.all_to_all(jnp.stack([pair_shard(low, high, is_low, 0)] * lax.axis_si...]
  transfers between devices with their start and end apart: 12 -> 12, of which waited for: 9 -> 8; matrix products, arithmetic and copies ran while one was open for 8% -> 10% of each run, Pallas kernels for 0% -> 0%
where the time goes in v1:
time: 631 us; the launch traced here: 630 us
  waiting for transfers between devices  512 us (81%)
  matrix products  43.5 us (7%)
  starting transfers between devices  27.3 us (4%)
  local copies, waits for them, and re-layouts  21.7 us (3%)
  between operations  14.3 us (2%)
  other arithmetic  11.1 us (2%)
    all_to_all x1, waiting for transfers between devices, local(): lax.all_to_all(jnp.stack([pair_shard(low, high, is_low, 0)] * lax.axis_si...  157 us
    all_gather x1, waiting for transfers between devices, local(): lax.all_gather(out_weight[0], ('xl', 'zl', 'dp'), axis=0, tiled=True)  113 us
    psum x1, waiting for transfers between devices, local(): lax.psum(grad_down[owners - 2 * half:].astype(jnp.bfloat16), ('xl', 'zl'))  84.6 us
    reduce_scatter x1, waiting for transfers between devices, local(): lax.psum_scatter(spread.astype(jnp.bfloat16), ('xl', 'zl'), scatter_dimen...  71.9 us
    ppermute x4, waiting for transfers between devices, swap_pair(): return lax.ppermute(block, 'xh', [(0, 1), (1, 0)])  60 us
    ppermute x1, waiting for transfers between devices, local(): other = lax.ppermute(source, ('xh', 'sec'), pairs)  18.9 us
  transfers between devices with their start and end apart: 12, of which 8 were waited for; matrix products, arithmetic and copies ran while one was open for 10% of the time, Pallas kernels for 0%

profile of v1, /device:TPU:8, one launch (start us, length us, event | category | flops | bytes accessed | tf_op | source)
XLA Modules:
  0.0 630.4 jit_solution(9816814272714296542)
XLA Ops:
  8.0 1.1 reshape_squeeze.6
  9.9 3.1 collective-permute-start.3
  13.0 5.9 collective-permute-done.3
  19.1 3.6 stack.2
  22.6 9.7 %all-to-all-start = ((bf16[16,96,2432]{2,1,0:T(8,128)(2,1)}), bf16[16,96,2432]{2,1,0:T(8,128)(2,1)}, u32[]{:S(2)}, u32[]{:S(2)}) async-start(bf16[16,96,2432]{2,1,0:T(8,128)(2,1)} %stack.2), calls=%async_computation | async-start | bytes 14942208 | tf_op jit(solution)/shard_map/all_to_all | solution.py:73
  32.5 2.8 collective-permute-start.1
  35.3 54.1 %collective-permute-done.1 = bf16[3,3,48,256]{3,2,1,0:T(8,128)(2,1)S(1)} collective-permute-done((bf16[3,3,48,256]{3,2,1,0:T(8,128)(2,1)S(1)}, bf16[3,3,48,256]{3,2,1,0:T(8,128)(2,1)S(1)}, u32[]{:S(2)}, u32[]{:S(2)}) %collective-permute-start.1) | collective-permute-done | bytes 221216 | tf_op jit(solution)/shard_map/ppermute | solution.py:26
  89.5 0.8 pad_maximum_fusion.3
  90.6 1.9 collective-permute-start
  92.6 18.9 %collective-permute-done.2 = bf16[256,1536]{1,0:T(8,128)(2,1)S(1)} collective-permute-done((bf16[256,1536]{1,0:T(8,128)(2,1)S(1)}, bf16[256,1536]{1,0:T(8,128)(2,1)S(1)}, u32[]{:S(2)}, u32[]{:S(2)}) %collective-permute-start.2) | collective-permute-done | bytes 786464 | tf_op jit(solution)/shard_map/ppermute | solution.py:95
  111.4 0.9 copy-done.7
  112.4 0.7 copy.174
  113.3 156.9 %all-to-all-done = bf16[16,96,2432]{2,1,0:T(8,128)(2,1)} async-done(((bf16[16,96,2432]{2,1,0:T(8,128)(2,1)}), bf16[16,96,2432]{2,1,0:T(8,128)(2,1)}, u32[]{:S(2)}, u32[]{:S(2)}) %all-to-all-start) | async-done | bytes 7471136 | tf_op jit(solution)/shard_map/all_to_all | solution.py:73
  270.1 6.9 %fusion.47 = f32[512,2432]{1,0:T(8,128)S(1)} fusion(bf16[512,1536]{0,1:T(8,128)(2,1)S(1)} %bitcast.116, bf16[1536,2432]{1,0:T(8,128)(2,1)} %bitcast.9), kind=kOutput, calls=%fused_computation.110 | convolution fusion | flops 3825205248 | bytes 14024704 | tf_op jit(solution)/shard_map/dot_general | solution.py:100
  277.0 2.0 fusion.44
  279.3 1.9 copy.184
  281.7 1.7 copy.182
  283.5 2.5 fusion.26
  286.0 1.1 fusion.24
  287.4 1.9 negate_convert_fusion
  289.2 0.9 fusion.23
  290.3 4.6 fusion.17
  294.9 5.3 fusion.16
  300.1 1.9 pad_maximum_fusion
  302.4 0.9 copy-done.6
  303.3 0.8 slice.126
  305.0 4.5 fusion.25
  309.5 5.6 fusion.11
  315.2 1.1 fusion.12
  316.3 112.6 %all-gather.6.cloned.1.call-done = bf16[1,768,1536]{2,1,0:T(8,128)(2,1)} async-done(((bf16[1,48,1536]{2,1,0:T(8,128)(2,1)}), bf16[1,768,1536]{2,1,0:T(8,128)(2,1)}) %all-gather.6.cloned.1.call-update) | async-done | bytes 2359312 | tf_op jit(solution)/shard_map/all_gather | solution.py:86
  428.9 3.3 fusion.3
  432.3 1.0 slice.169
  433.2 3.0 collective-permute-start.4
  436.3 71.9 %reduce-scatter.2.cloned.1.call-done = bf16[1,768,256]{2,1,0:T(8,128)(2,1)} async-done(((bf16[8,768,256]{2,1,0:T(8,128)(2,1)}), bf16[1,768,256]{2,1,0:T(8,128)(2,1)}) %reduce-scatter.2.cloned.1.call-update) | async-done | bytes 393232 | tf_op jit(solution)/shard_map/reduce_scatter | solution.py:128
  508.1 1.8 constant_dynamic-update-slice_fusion.1
  509.9 84.6 %all-reduce.3.cloned.1.call-done = bf16[1,768,256]{2,1,0:T(8,128)(2,1)} async-done(((bf16[1,768,256]{2,1,0:T(8,128)(2,1)}), bf16[1,768,256]{2,1,0:T(8,128)(2,1)}) %all-reduce.3.cloned.1.call-update) | async-done | bytes 393232 | tf_op jit(solution)/shard_map/psum | solution.py:127
  594.5 1.8 constant_dynamic-update-slice_fusion
  596.3 1.9 select_reduce_fusion
  598.2 0.8 fusion.22
  600.5 0.7 fusion.21
  601.8 1.6 fusion.18
  604.2 2.7 collective-permute-start.5
  606.9 0.8 copy.194
  607.7 3.6 all-to-all-start.1
  611.3 2.5 fusion.32
  613.8 0.8 bitcast_select_fusion.2
  614.7 7.5 %all-to-all-done.1 = bf16[16,48,256]{2,1,0:T(8,128)(2,1)S(1)} async-done(((bf16[16,48,256]{2,1,0:T(8,128)(2,1)}), bf16[16,48,256]{2,1,0:T(8,128)(2,1)S(1)}, u32[]{:S(2)}, u32[]{:S(2)}) %all-to-all-start.1) | async-done | bytes 393248 | tf_op jit(solution)/shard_map/all_to_all | solution.py:136
  622.8 1.1 subtract_multiply_fusion
  (77 shorter events, 8.4 us)
Async XLA Ops:
  9.9 9.0 %collective-permute-start.3 = (bf16[48,2432]{1,0:T(8,128)(2,1)S(1)}, bf16[48,2432]{1,0:T(8,128)(2,1)S(1)}, u32[]{:S(2)}, u32[]{:S(2)}) collective-permute-start(bf16[48,2432]{1,0:T(8,128)(2,1)S(1)} %broadcast_select_fusion.2), channel_id=1, source_target_pairs={{0,128},{128,0},{1,129},{129,1},{2,130},{130,2},{3,131},{131,3},{4... | collective-permute-start | bytes 700424 | tf_op jit(solution)/shard_map/ppermute | solution.py:26
  22.6 9.7 %copy-start.1 = (f32[1,1,3,6,48,256]{5,4,3,2,1,0:T(8,128)S(1)}, f32[1,1,3,6,48,256]{5,4,3,2,1,0:T(8,128)}, u32[]{:S(2)}) copy-start(f32[1,1,3,6,48,256]{5,4,3,2,1,0:T(8,128)} %param.11) | copy-start | bytes 2654212
  22.6 247.5 %all-to-all-start = ((bf16[16,96,2432]{2,1,0:T(8,128)(2,1)}), bf16[16,96,2432]{2,1,0:T(8,128)(2,1)}, u32[]{:S(2)}, u32[]{:S(2)}) async-start(bf16[16,96,2432]{2,1,0:T(8,128)(2,1)} %stack.2), calls=%async_computation | async-start | bytes 14942208 | tf_op jit(solution)/shard_map/all_to_all | solution.py:73
  32.3 251.1 %all-gather.4.cloned.1.call-start = ((), (), s32[]{:S(2)}) async-start(), calls=%async_computation.3 | async-start | bytes 3981312 | tf_op jit(solution)/shard_map/all_gather | solution.py:83
  32.4 57.9 %copy-start.8 = (bf16[1,1,256,1536]{3,2,1,0:T(8,128)(2,1)S(1)}, bf16[1,1,256,1536]{3,2,1,0:T(8,128)(2,1)}, u32[]{:S(2)}) copy-start(bf16[1,1,256,1536]{3,2,1,0:T(8,128)(2,1)} %param.7) | copy-start | bytes 2359300
  32.4 57.9 %copy-start.9 = (bf16[1,256,1536]{2,1,0:T(8,128)(2,1)S(1)}, bf16[1,256,1536]{2,1,0:T(8,128)(2,1)}, u32[]{:S(2)}) copy-start(bf16[1,256,1536]{2,1,0:T(8,128)(2,1)} %param.6) | copy-start | bytes 2359300
  32.5 56.9 %collective-permute-start.1 = (bf16[3,3,48,256]{3,2,1,0:T(8,128)(2,1)S(1)}, bf16[3,3,48,256]{3,2,1,0:T(8,128)(2,1)S(1)}, u32[]{:S(2)}, u32[]{:S(2)}) collective-permute-start(bf16[3,3,48,256]{3,2,1,0:T(8,128)(2,1)S(1)} %broadcast_select_fusion.6), channel_id=1, source_target_pairs={{0,128},{128,0},{1,129},{129,1},{2,130},{130,2},{3,131},{131,3},{4... | collective-permute-start | bytes 663560 | tf_op jit(solution)/shard_map/ppermute | solution.py:26
  90.3 338.6 %all-gather.6.cloned.1.call-start = ((), (), s32[]{:S(2)}) async-start(), calls=%async_computation.6 | async-start | bytes 2506752 | tf_op jit(solution)/shard_map/all_gather | solution.py:86
  90.5 20.9 %collective-permute-start.2 = (bf16[256,1536]{1,0:T(8,128)(2,1)S(1)}, bf16[256,1536]{1,0:T(8,128)(2,1)S(1)}, u32[]{:S(2)}, u32[]{:S(2)}) collective-permute-start(bf16[256,1536]{1,0:T(8,128)(2,1)S(1)} %bitcast_select_fusion), channel_id=1, source_target_pairs={{0,130},{2,132},{4,134},{6,136},{8,138},{10,140},{12,142},{14,128}... | collective-permute-start | bytes 2359304 | tf_op jit(solution)/shard_map/ppermute | solution.py:95
  90.6 20.8 %collective-permute-start = (bf16[256,1536]{1,0:T(8,128)(2,1)S(1)}, bf16[256,1536]{1,0:T(8,128)(2,1)S(1)}, u32[]{:S(2)}, u32[]{:S(2)}) collective-permute-start(bf16[256,1536]{1,0:T(8,128)(2,1)S(1)} %bitcast_select_fusion), channel_id=1, source_target_pairs={{0,2},{2,4},{4,6},{6,8},{8,10},{10,12},{12,14},{14,0},{1,3},{3,5},... | collective-permute-start | bytes 2359304 | tf_op jit(solution)/shard_map/ppermute | solution.py:89
  92.5 415.6 %reduce-scatter.2.cloned.1.call-start = ((), (), s32[]{:S(2)}) async-start(), calls=%async_computation.4 | async-start | bytes 3538944 | tf_op jit(solution)/shard_map/reduce_scatter | solution.py:128
  111.4 0.9 copy-start.7
  283.4 2.5 copy-start.11
  286.0 1.4 copy-start.4
  287.0 2.2 copy-start.12
  289.2 1.1 copy-start.5
  294.9 5.3 slice-start
  302.0 1.3 copy-start.6
  302.0 2.1 copy-start.3
  302.0 292.5 %all-reduce.3.cloned.1.call-start = ((), (), s32[]{:S(2)}) async-start(), calls=%async_computation.5 | async-start | bytes 786432 | tf_op jit(solution)/shard_map/psum | solution.py:127
  433.2 178.1 %collective-permute-start.4 = (bf16[256,1536]{1,0:T(8,128)(2,1)}, bf16[256,1536]{1,0:T(8,128)(2,1)}, u32[]{:S(2)}, u32[]{:S(2)}) collective-permute-start(bf16[256,1536]{1,0:T(8,128)(2,1)} %slice.169), channel_id=1, source_target_pairs={{0,128},{128,0},{1,129},{129,1},{2,130},{130,2},{3,131},{131,3},{4... | collective-permute-start | bytes 2359304 | tf_op jit(solution)/shard_map/ppermute | solution.py:26
  600.4 1.4 copy-start
  603.5 4.2 copy-start.10
  604.2 9.6 %collective-permute-start.5 = (bf16[1,48,256]{2,1,0:T(8,128)(2,1)}, bf16[1,48,256]{2,1,0:T(8,128)(2,1)}, u32[]{:S(2)}, u32[]{:S(2)}) collective-permute-start(bf16[1,48,256]{2,1,0:T(8,128)(2,1)} %select_bitcast_fusion), channel_id=1, source_target_pairs={{0,128},{128,0},{1,129},{129,1},{2,130},{130,2},{3,131},{131,3},{4... | collective-permute-start | bytes 73736 | tf_op jit(solution)/shard_map/ppermute | solution.py:26
  607.7 14.4 %all-to-all-start.1 = ((bf16[16,48,256]{2,1,0:T(8,128)(2,1)}), bf16[16,48,256]{2,1,0:T(8,128)(2,1)S(1)}, u32[]{:S(2)}, u32[]{:S(2)}) async-start(bf16[16,48,256]{2,1,0:T(8,128)(2,1)} %bitcast.21), calls=%async_computation.2 | async-start | bytes 786432 | tf_op jit(solution)/shard_map/all_to_all | solution.py:136
  614.6 7.7 %copy-start.2 = (f32[1,1,3,6,48,256]{5,4,3,2,1,0:T(8,128)S(1)}, f32[1,1,3,6,48,256]{5,4,3,2,1,0:T(8,128)}, u32[]{:S(2)}) copy-start(f32[1,1,3,6,48,256]{5,4,3,2,1,0:T(8,128)} %param.11) | copy-start | bytes 2654212
Sparse Core Ops, SparseCore 0:
  90.4 190.4 all-gather.3
  282.7 146.1 all-gather.5
  431.5 76.6 reduce-scatter.1
  510.6 83.8 all-reduce.2
